TPU v7x, 256 devices: a whole 4x4x8 slice. The times are simulated.
256 devices in a mesh: dp: 8 (over x, core), expert: 32 (over z, y).
Axes of the slice: x: 4, y: 4, z: 8, core: 2. Of those that a mesh axis runs over, the one named last changes fastest.
Arguments:
- tokens: bfloat16 [4096, 2880], P(('dp', 'expert')), may hold values from -200 to 200
- norm_gain: float32 [2880], replicated, may hold values from 0.5 to 4
- router_weight: bfloat16 [2880, 32], replicated, may hold values from -0.02734375 to 0.02734375
- router_bias: float32 [32], replicated, may hold values from -1 to 1
- expert_ids: int32 [4096, 4], P(('dp', 'expert')), may hold values from 0 to 31, all different within a row; in each aligned block of 16 rows (0 to 15, 16 to 31, ...) at most 4 rows name the same one
- placement: int32 [32], replicated, may hold values from 0 to 31, each once
- gate_up: bfloat16 [32, 2, 2880, 2880], P('expert', None, None, 'dp'), may hold values from -0.109375 to 0.109375
- gate_up_bias: float32 [32, 2, 2880], P('expert', None, 'dp'), may hold values from -3 to 3
- down_proj: bfloat16 [32, 2880, 2880], P('expert', 'dp'), may hold values from -0.109375 to 0.109375
- down_bias: float32 [32, 2880], replicated, may hold values from -3 to 3
Outputs:
- mixed: bfloat16 [4096, 2880], P(('dp', 'expert'))
Inputs may be any that keep to these rules, and one draw needn't show every extreme that they name: `expert_ids`: in the rows of one device no expert is named more than 4 times; in every draw some device names some expert exactly 4 times. `placement`: every holder index appears once.
All inputs are finite; a program needn't handle non-finite values.
Results may differ from a plain program's by a relative error of at most 0.015.
Values may be sent and summed in bfloat16 or wider, within the bound.
A program may use at most 64 MiB of HBM per device.

v0:
```python
import jax
import jax.numpy as jnp
from jax import lax
from jax.sharding import PartitionSpec as P
from jax.experimental.layout import Layout, with_layout_constraint

TOPK = 4
EPS = 1e-05
LIMIT = 7.0
ALPHA = 1.702


def normalize(tokens, norm_gain):
    values = tokens.astype(jnp.float32)
    mean_square = jnp.mean(values * values, axis=-1, keepdims=True)
    return (values * lax.rsqrt(mean_square + EPS) * norm_gain).astype(jnp.bfloat16)


def routing(normed, router_weight, router_bias, expert_ids):
    logits = jnp.dot(normed, router_weight, preferred_element_type=jnp.float32) + router_bias
    expert_range = jnp.arange(logits.shape[1], dtype=jnp.int32)
    matches = expert_ids[:, :, None] == expert_range[None, None, :]
    picked = jnp.sum(jnp.where(matches, logits[:, None, :], 0.0), axis=2)
    powers = jnp.exp(picked)
    return powers / jnp.sum(powers, axis=1, keepdims=True)


def lookup(expert_ids, placement):
    return jnp.take(placement, expert_ids, mode="clip")


def slot_positions(columns, experts):
    flat_ids = columns.reshape(-1)
    order = jnp.arange(flat_ids.shape[0], dtype=jnp.int32)
    earlier = (flat_ids[:, None] == flat_ids[None, :]) & (order[None, :] < order[:, None])
    return jnp.sum(earlier.astype(jnp.int32), axis=1).reshape(columns.shape)


def swiglu(gate_value, up_value):
    gate_value = jnp.minimum(gate_value, LIMIT)
    up_value = jnp.clip(up_value, -LIMIT, LIMIT)
    return (up_value + 1.0) * gate_value * jax.nn.sigmoid(ALPHA * gate_value)


def body(
    tokens,
    norm_gain,
    router_weight,
    router_bias,
    expert_ids,
    placement,
    gate_up,
    gate_up_bias,
    down_proj,
    down_bias,
):
    tok_dev = tokens.shape[0]
    model_width = tokens.shape[1]
    experts = placement.shape[0]
    capacity = max(2, 2 * tok_dev * TOPK // experts)
    expert_count = lax.axis_size("expert")
    dp_count = lax.axis_size("dp")
    normed = normalize(tokens, norm_gain)
    weights = routing(normed, router_weight, router_bias, expert_ids)
    columns = lookup(expert_ids, placement)
    slots = slot_positions(columns, experts)
    target_row = columns * capacity + slots
    targets = jnp.arange(experts * capacity, dtype=jnp.int32)
    dispatch = jnp.sum(
        (target_row[:, :, None] == targets[None, None, :]).astype(jnp.int32), axis=1
    ).astype(jnp.bfloat16)
    outgoing = jnp.dot(dispatch.T, normed, preferred_element_type=jnp.float32).astype(jnp.bfloat16)
    outgoing = with_layout_constraint(outgoing, Layout(major_to_minor=(0, 1)))
    outgoing = outgoing.reshape(experts, capacity, model_width)
    gate_weight = gate_up[0, 0]
    up_weight = gate_up[0, 1]
    gate_bias = gate_up_bias[0, 0]
    up_bias = gate_up_bias[0, 1]
    down_weight = down_proj[0]
    group_width = gate_weight.shape[1]
    row_block = lax.all_to_all(outgoing, "expert", split_axis=0, concat_axis=0, tiled=True)
    row_block = row_block.reshape(experts * capacity, model_width)
    flat_rows = lax.all_gather(row_block, "dp", axis=0, tiled=True)
    gate_value = jnp.dot(flat_rows, gate_weight, preferred_element_type=jnp.float32) + gate_bias
    up_value = jnp.dot(flat_rows, up_weight, preferred_element_type=jnp.float32) + up_bias
    hidden = swiglu(gate_value, up_value).astype(jnp.bfloat16)
    hidden = hidden.reshape(dp_count, -1, hidden.shape[-1])
    partials = jnp.einsum("grf,fo->gro", hidden, down_weight, preferred_element_type=jnp.float32)
    partials = partials.astype(jnp.bfloat16)
    partials = with_layout_constraint(partials, Layout(major_to_minor=(0, 1, 2)))
    partials = partials.reshape(-1, model_width)
    reduced_parts = lax.psum_scatter(partials, "dp", scatter_dimension=0, tiled=True)
    reduced_parts = reduced_parts.reshape(expert_count, capacity, model_width)
    reduced = lax.all_to_all(reduced_parts, "expert", split_axis=0, concat_axis=0, tiled=True)
    reduced = reduced.reshape(experts, capacity, model_width)
    picked = reduced[columns.T, slots.T].astype(jnp.float32) + down_bias[columns.T]
    picked = picked.astype(jnp.bfloat16).astype(jnp.float32)
    return jnp.sum(weights.T[:, :, None] * picked, axis=0).astype(jnp.bfloat16)


def solution(mesh):
    return jax.shard_map(
        body,
        mesh=mesh,
        in_specs=(
            P(("dp", "expert"), None),
            P(),
            P(),
            P(),
            P(("dp", "expert"), None),
            P(),
            P("expert", None, None, "dp"),
            P("expert", None, "dp"),
            P("expert", "dp", None),
            P(),
        ),
        out_specs=P(("dp", "expert"), None),
        check_vma=False,
    )
```

profile of v0, /device:TPU:8, one launch (start us, length us, event | category | flops | bytes accessed | tf_op | source)
XLA Modules:
  0.0 188.9 jit_solution(12569673349516595402)
XLA Ops:
  6.5 0.9 copy.21
  7.5 0.1 reshape.52
  7.6 0.8 gather_fusion
  8.4 0.2 convert_reduce_fusion.1
  8.6 0.1 reshape.51
  8.6 0.1 reshape.44
  8.7 0.1 copy.22
  8.8 0.1 convert_reduce_fusion
  8.9 0.1 fusion.15
  9.1 0.4 convolution_convert_fusion.1
  9.5 1.0 reshape.45
  10.5 33.6 %all_to_all.10 = bf16[32,4,2880]{2,1,0:T(4,128)(2,1)S(1)} all-to-all(bf16[32,4,2880]{2,1,0:T(4,128)(2,1)} %reshape.45), channel_id=1, replica_groups=mesh['dp'=8,'expert'=32] {'expert'}, dimensions={0} | all-to-all | bytes 1474560 | tf_op jit(solution)/shard_map/all_to_all | solution.py:81
  44.1 1.2 reshape.46
  45.4 0.0 reduce-scatter.2.cloned.1.call-start
  45.5 39.1 %all-gather.2.cloned.1.call-done = bf16[1024,2880]{1,0:T(8,128)(2,1)} async-done(((bf16[128,2880]{1,0:T(8,128)(2,1)}), bf16[1024,2880]{1,0:T(8,128)(2,1)}) %all-gather.2.cloned.1.call-update) | async-done | bytes 5898256 | tf_op jit(solution)/shard_map/all_gather | solution.py:83
  84.6 6.0 %fusion.1 = f32[1024,360]{0,1:T(8,128)S(1)} fusion(bf16[1024,2880]{1,0:T(8,128)(2,1)} %all-gather.2.cloned.1.call-done, bf16[1,2,2880,360]{2,3,1,0:T(8,128)(2,1)} %param.16), kind=kOutput, calls=%fused_computation.6 | convolution fusion | flops 2123366400 | bytes 9623552 | tf_op jit(solution)/shard_map/dot_general | solution.py:84
  90.5 4.4 %fusion.9 = bf16[45,8,8,128]{3,2,1,0:T(8,128)(2,1)S(1)} fusion(f32[1024,360]{0,1:T(8,128)S(1)} %fusion.1, bf16[1024,2880]{1,0:T(8,128)(2,1)S(1)} %copy-done.7, bf16[1,2,2880,360]{2,3,1,0:T(8,128)(2,1)} %param.16, f32[360]{0:T(512)S(1)} %get-tuple-element.6, f32[360]{0:T(512)S(1)} %get-tuple-element.5), kind=kOutput, calls=%fused_computation.13 | convolution fusion | flops 2127790080 | bytes 10232640 | tf_op jit(solution)/shard_map/dot_general | solution.py:85
  95.0 5.4 %convolution_convert_fusion = bf16[8,128,2880]{2,1,0:T(8,128)(2,1)} fusion(bf16[1,360,2880]{2,1,0:T(8,128)(2,1)S(1)} %copy-done, bf16[45,8,8,128]{3,2,1,0:T(8,128)(2,1)S(1)} %fusion.9), kind=kOutput, calls=%fused_computation.3 | convolution fusion | flops 2126315520 | bytes 8709120 | tf_op jit(solution)/shard_map/grf,fo->gro/dot_general | solution.py:88
  100.5 44.3 %reduce-scatter.2.cloned.1.call-done = bf16[128,2880]{1,0:T(8,128)(2,1)} async-done(((bf16[1024,2880]{1,0:T(8,128)(2,1)}), bf16[128,2880]{1,0:T(8,128)(2,1)}) %reduce-scatter.2.cloned.1.call-update) | async-done | bytes 737296 | tf_op jit(solution)/shard_map/reduce_scatter | solution.py:92
  144.8 2.4 %reshape.49 = bf16[32,4,2880]{2,1,0:T(4,128)(2,1)} reshape(bf16[128,2880]{1,0:T(8,128)(2,1)} %reduce-scatter.2.cloned.1.call-done) | data formatting | bytes 1474560 | tf_op jit(solution)/shard_map/reshape | solution.py:93
  147.1 10.3 %all-to-all-start.1 = ((bf16[32,4,2880]{2,1,0:T(4,128)(2,1)}), bf16[32,4,2880]{2,1,0:T(4,128)(2,1)S(1)}, u32[]{:S(2)}, u32[]{:S(2)}) async-start(bf16[32,4,2880]{2,1,0:T(4,128)(2,1)} %reshape.49), calls=%async_computation.2 | async-start | bytes 1507328 | tf_op jit(solution)/shard_map/all_to_all | solution.py:94
  157.5 0.1 copy.24
  157.6 0.1 reshape.58
  157.6 0.1 copy.25
  157.7 0.1 reshape.66
  157.9 1.7 gather_fusion.2
  159.6 1.1 convolution_add_fusion
  160.7 0.2 select_reduce_fusion
  160.9 17.3 %all-to-all-done.1 = bf16[32,4,2880]{2,1,0:T(4,128)(2,1)S(1)} async-done(((bf16[32,4,2880]{2,1,0:T(4,128)(2,1)}), bf16[32,4,2880]{2,1,0:T(4,128)(2,1)S(1)}, u32[]{:S(2)}, u32[]{:S(2)}) %all-to-all-start.1) | async-done | bytes 737312 | tf_op jit(solution)/shard_map/all_to_all | solution.py:94
  178.2 1.8 gather_fusion.1
  180.1 1.2 add_convert_fusion
  181.3 0.8 fusion.12
  (29 shorter events, 0.2 us)
Async XLA Ops:
  6.5 88.5 %copy-start = (bf16[1,360,2880]{2,1,0:T(8,128)(2,1)S(1)}, bf16[1,360,2880]{2,1,0:T(8,128)(2,1)}, u32[]{:S(2)}) copy-start(bf16[1,360,2880]{2,1,0:T(8,128)(2,1)} %param.18) | copy-start | bytes 6220804
  6.5 1.0 copy-start.1
  6.5 78.0 %all-gather.2.cloned.1.call-start = ((), (), s32[]{:S(2)}) async-start(), calls=%async_computation.3 | async-start | bytes 6782976 | tf_op jit(solution)/shard_map/all_gather | solution.py:83
  7.6 1.3 copy-start.3
  7.6 1.5 copy-start.4
  10.5 34.9 %copy-start.6 = (f32[1,2,360]{2,1,0:T(2,128)S(1)}, f32[1,2,360]{2,1,0:T(2,128)}, u32[]{:S(2)}) copy-start(f32[1,2,360]{2,1,0:T(2,128)} %param.17) | copy-start | bytes 8644
  45.4 99.4 %reduce-scatter.2.cloned.1.call-start = ((), (), s32[]{:S(2)}) async-start(), calls=%async_computation.4 | async-start | bytes 6782976 | tf_op jit(solution)/shard_map/reduce_scatter | solution.py:92
  84.5 6.0 %copy-start.7 = (bf16[1024,2880]{1,0:T(8,128)(2,1)S(1)}, bf16[1024,2880]{1,0:T(8,128)(2,1)}, u32[]{:S(2)}) copy-start(bf16[1024,2880]{1,0:T(8,128)(2,1)} %all-gather.2.cloned.1.call-done) | copy-start | bytes 17694724
  100.5 57.4 %copy-start.2 = (f32[32,2880]{1,0:T(8,128)S(1)}, f32[32,2880]{1,0:T(8,128)}, u32[]{:S(2)}) copy-start(f32[32,2880]{1,0:T(8,128)} %param.19) | copy-start | bytes 1105924
  147.1 31.1 %all-to-all-start.1 = ((bf16[32,4,2880]{2,1,0:T(4,128)(2,1)}), bf16[32,4,2880]{2,1,0:T(4,128)(2,1)S(1)}, u32[]{:S(2)}, u32[]{:S(2)}) async-start(bf16[32,4,2880]{2,1,0:T(4,128)(2,1)} %reshape.49), calls=%async_computation.2 | async-start | bytes 1507328 | tf_op jit(solution)/shard_map/all_to_all | solution.py:94
  157.8 1.7 copy-start.8
  157.8 2.9 %copy-start.5 = (s32[16,4]{0,1:T(4,128)S(1)}, s32[16,4]{0,1:T(4,128)}, u32[]{:S(2)}) copy-start(s32[16,4]{0,1:T(4,128)} %param.14) | copy-start | bytes 772
Sparse Core Ops, SparseCore 0:
  45.5 39.0 all-gather.1
  100.6 44.1 reduce-scatter.1
where the time goes:
time: 189 us
  waiting for transfers between devices  101 us (53%)
  blocking collectives  33.6 us (18%)
  matrix products  17.4 us (9%)
  between operations  13.6 us (7%)
  local copies, waits for them, and re-layouts  10.6 us (6%)
  starting transfers between devices  10.4 us (6%)
  other arithmetic  2.61 us (1%)
    reduce_scatter x1, waiting for transfers between devices, body(): lax.psum_scatter(partials, 'dp', scatter_dimension=0, tiled=True)  44.3 us
    all_gather x1, waiting for transfers between devices, body(): flat_rows = lax.all_gather(row_block, 'dp', axis=0, tiled=True)  39.1 us
    all_to_all x1, blocking collectives, body(): lax.all_to_all(outgoing, 'expert', split_axis=0, concat_axis=0, tiled=True)  33.6 us
    all_to_all x1, waiting for transfers between devices, body(): lax.all_to_all(reduced_parts, 'expert', split_axis=0, concat_axis=0, tile...  17.3 us
    all_to_all x1, starting transfers between devices, body(): lax.all_to_all(reduced_parts, 'expert', split_axis=0, concat_axis=0, tile...  10.3 us
    dot_general x1, matrix products, body(): jnp.dot(flat_rows, gate_weight, preferred_element_type=jnp.float32)  5.98 us
    dot_general x1, matrix products, body(): jnp.einsum('grf,fo->gro', hidden, down_weight, preferred_element_type=jnp...  5.42 us
    dot_general x1, matrix products, body(): jnp.dot(flat_rows, up_weight, preferred_element_type=jnp.float32) + up_bias  4.45 us
  transfers between devices with their start and end apart: 3, of which 3 were waited for; matrix products, arithmetic and copies ran while one was open for 2% of the time, Pallas kernels for 0%

commit v1 on v0

--- a/solution.py
+++ b/solution.py
@@ -1,3 +1,4 @@
+import functools
 import jax
 import jax.numpy as jnp
 from jax import lax
@@ -8,6 +9,17 @@
 EPS = 1e-05
 LIMIT = 7.0
 ALPHA = 1.702
+
+
+def link_squares(u_in, across):
+    after = jnp.concatenate(
+        lax.all_to_all(jnp.stack([u_in for _ in range(lax.axis_size(across))]), across, 0, 0),
+        axis=0,
+    )
+    return after
+
+
+_register_group = functools.partial(link_squares, across="dp")
 
 
 def normalize(tokens, norm_gain):
@@ -80,7 +92,7 @@
     group_width = gate_weight.shape[1]
     row_block = lax.all_to_all(outgoing, "expert", split_axis=0, concat_axis=0, tiled=True)
     row_block = row_block.reshape(experts * capacity, model_width)
-    flat_rows = lax.all_gather(row_block, "dp", axis=0, tiled=True)
+    flat_rows = _register_group(row_block)
     gate_value = jnp.dot(flat_rows, gate_weight, preferred_element_type=jnp.float32) + gate_bias
     up_value = jnp.dot(flat_rows, up_weight, preferred_element_type=jnp.float32) + up_bias
     hidden = swiglu(gate_value, up_value).astype(jnp.bfloat16)

time: 189 us -> 230 us (1.22)
  waiting for transfers between devices: 101 us -> 124 us
  local copies, waits for them, and re-layouts: 10.6 us -> 24.1 us
  starting transfers between devices: 10.4 us -> 15 us
    all_to_all x0 -> x1, waiting for transfers between devices: none -> 67.8 us  [link_squares(): lax.all_to_all(jnp.stack([u_in for _ in range(lax.axis_size(across))]), a...]
    all_gather x1 -> x0, waiting for transfers between devices: 39.1 us -> none  [body(): flat_rows = lax.all_gather(row_block, 'dp', axis=0, tiled=True)]
    all_to_all x0 -> x1, local copies, waits for them, and re-layouts: none -> 8.45 us  [link_squares(): lax.all_to_all(jnp.stack([u_in for _ in range(lax.axis_size(across))]), a...]
    another operation x0 -> x3, local copies, waits for them, and re-layouts: none -> 6 us  [link_squares(): jnp.stack([u_in for _ in range(lax.axis_size(across))])]
    reduce_scatter x1, waiting for transfers between devices: 44.3 us -> 39.1 us  [body(): lax.psum_scatter(partials, 'dp', scatter_dimension=0, tiled=True)]
    all_to_all x0 -> x1, starting transfers between devices: none -> 4.85 us  [link_squares(): lax.all_to_all(jnp.stack([u_in for _ in range(lax.axis_size(across))]), a...]
  transfers between devices with their start and end apart: 3 -> 3, of which waited for: 3 -> 3; matrix products, arithmetic and copies ran while one was open for 2% -> 1% of each run, Pallas kernels for 0% -> 0%
where the time goes in v1:
time: 230 us; the launch traced here: 229 us
  waiting for transfers between devices  124 us (54%)
  blocking collectives  33.4 us (15%)
  local copies, waits for them, and re-layouts  24.1 us (10%)
  matrix products  15.8 us (7%)
  starting transfers between devices  15 us (7%)
  between operations  13.6 us (6%)
  other arithmetic  2.61 us (1%)
    all_to_all x1, waiting for transfers between devices, link_squares(): lax.all_to_all(jnp.stack([u_in for _ in range(lax.axis_size(across))]), a...  67.8 us
    reduce_scatter x1, waiting for transfers between devices, body(): lax.psum_scatter(partials, 'dp', scatter_dimension=0, tiled=True)  39.1 us
    all_to_all x1, blocking collectives, body(): lax.all_to_all(outgoing, 'expert', split_axis=0, concat_axis=0, tiled=True)  33.4 us
    all_to_all x1, waiting for transfers between devices, body(): lax.all_to_all(reduced_parts, 'expert', split_axis=0, concat_axis=0, tile...  17.5 us
    all_to_all x1, starting transfers between devices, body(): lax.all_to_all(reduced_parts, 'expert', split_axis=0, concat_axis=0, tile...  10.1 us
    all_to_all x1, local copies, waits for them, and re-layouts, link_squares(): lax.all_to_all(jnp.stack([u_in for _ in range(lax.axis_size(across))]), a...  8.45 us
    another operation x3, local copies, waits for them, and re-layouts, link_squares(): jnp.stack([u_in for _ in range(lax.axis_size(across))])  6 us
    dot_general x1, matrix products, body(): jnp.dot(flat_rows, gate_weight, preferred_element_type=jnp.float32)  5.98 us
  transfers between devices with their start and end apart: 3, of which 3 were waited for; matrix products, arithmetic and copies ran while one was open for 1% of the time, Pallas kernels for 0%

profile of v1, /device:TPU:8, one launch (start us, length us, event | category | flops | bytes accessed | tf_op | source)
XLA Modules:
  0.0 229.0 jit_solution(13551698982978328477)
XLA Ops:
  6.5 0.9 copy.34
  7.5 0.1 reshape.54
  7.6 0.8 gather_fusion
  8.4 0.2 convert_reduce_fusion.1
  8.6 0.1 reshape.46
  8.7 0.1 copy.35
  8.9 0.1 fusion.15
  9.1 0.4 convolution_convert_fusion.1
  9.5 1.0 reshape.47
  10.5 33.4 %all_to_all.15 = bf16[32,4,2880]{2,1,0:T(4,128)(2,1)S(1)} all-to-all(bf16[32,4,2880]{2,1,0:T(4,128)(2,1)} %reshape.47), channel_id=1, replica_groups=mesh['dp'=8,'expert'=32] {'expert'}, dimensions={0} | all-to-all | bytes 1474560 | tf_op jit(solution)/shard_map/all_to_all | solution.py:93
  44.0 1.2 stack_reshape.2
  45.2 1.5 copy.36
  46.7 3.3 %stack.3 = bf16[8,128,2880]{1,2,0:T(8,128)(2,1)} broadcast(bf16[128,2880]{0,1:T(8,128)(2,1)S(1)} %copy.36), dimensions={1,2} | broadcast | bytes 6635520 | tf_op jit(solution)/shard_map/stack | solution.py:16
  50.0 4.8 %all-to-all-start.1 = ((bf16[8,128,2880]{1,2,0:T(8,128)(2,1)}), bf16[8,128,2880]{1,2,0:T(8,128)(2,1)}, u32[]{:S(2)}, u32[]{:S(2)}) async-start(bf16[8,128,2880]{1,2,0:T(8,128)(2,1)} %stack.3), calls=%async_computation.1 | async-start | bytes 11796480 | tf_op jit(solution)/shard_map/all_to_all | solution.py:16
  54.9 67.8 %all-to-all-done.1 = bf16[8,128,2880]{1,2,0:T(8,128)(2,1)} async-done(((bf16[8,128,2880]{1,2,0:T(8,128)(2,1)}), bf16[8,128,2880]{1,2,0:T(8,128)(2,1)}, u32[]{:S(2)}, u32[]{:S(2)}) %all-to-all-start.1) | async-done | bytes 5898272 | tf_op jit(solution)/shard_map/all_to_all | solution.py:16
  122.7 8.4 %copy.37 = bf16[8,128,2880]{2,1,0:T(8,128)(2,1)} copy(bf16[8,128,2880]{1,2,0:T(8,128)(2,1)} %all-to-all-done.1) | data formatting | bytes 11796480 | tf_op jit(solution)/shard_map/all_to_all | solution.py:16
  131.2 6.0 %fusion.1 = f32[1024,360]{0,1:T(8,128)S(1)} fusion(bf16[1024,2880]{1,0:T(8,128)(2,1)} %bitcast.35, bf16[1,2,2880,360]{2,3,1,0:T(8,128)(2,1)} %param.16), kind=kOutput, calls=%fused_computation.6 | convolution fusion | flops 2123366400 | bytes 9623552 | tf_op jit(solution)/shard_map/dot_general | solution.py:96
  137.2 0.3 slice-done.1
  137.5 2.9 %fusion.9 = bf16[45,8,8,128]{3,2,1,0:T(8,128)(2,1)S(1)} fusion(f32[1024,360]{0,1:T(8,128)S(1)} %fusion.1, bf16[1024,2880]{1,0:T(8,128)(2,1)S(1)} %bitcast.36, bf16[1,2,2880,360]{2,3,1,0:T(8,128)(2,1)S(1)} %bitcast.39, f32[360]{0:T(512)S(1)} %get-tuple-element.6, f32[360]{0:T(512)S(1)} %get-tuple-element.5), kind=kOutput, calls=%fused_computation.13 | convolution fusion | flops 2127790080 | bytes 10364928 | tf_op jit(solution)/shard_map/dot_general | solution.py:97
  140.4 5.4 %convolution_convert_fusion = bf16[8,128,2880]{2,1,0:T(8,128)(2,1)} fusion(bf16[1,360,2880]{2,1,0:T(8,128)(2,1)S(1)} %copy-done, bf16[45,8,8,128]{3,2,1,0:T(8,128)(2,1)S(1)} %fusion.9), kind=kOutput, calls=%fused_computation.3 | convolution fusion | flops 2126315520 | bytes 8709120 | tf_op jit(solution)/shard_map/grf,fo->gro/dot_general | solution.py:100
  145.8 39.1 %reduce-scatter.2.cloned.1.call-done = bf16[128,2880]{1,0:T(8,128)(2,1)} async-done(((bf16[1024,2880]{1,0:T(8,128)(2,1)}), bf16[128,2880]{1,0:T(8,128)(2,1)}) %reduce-scatter.2.cloned.1.call-update) | async-done | bytes 737296 | tf_op jit(solution)/shard_map/reduce_scatter | solution.py:104
  185.0 2.4 %reshape.51 = bf16[32,4,2880]{2,1,0:T(4,128)(2,1)} reshape(bf16[128,2880]{1,0:T(8,128)(2,1)} %reduce-scatter.2.cloned.1.call-done) | data formatting | bytes 1474560 | tf_op jit(solution)/shard_map/reshape | solution.py:105
  187.3 10.1 %all-to-all-start.2 = ((bf16[32,4,2880]{2,1,0:T(4,128)(2,1)}), bf16[32,4,2880]{2,1,0:T(4,128)(2,1)S(1)}, u32[]{:S(2)}, u32[]{:S(2)}) async-start(bf16[32,4,2880]{2,1,0:T(4,128)(2,1)} %reshape.51), calls=%async_computation.3 | async-start | bytes 1507328 | tf_op jit(solution)/shard_map/all_to_all | solution.py:106
  197.5 0.1 reshape.60
  197.7 0.1 reshape.68
  197.8 1.7 gather_fusion.2
  199.5 1.1 convolution_add_fusion
  200.7 0.2 select_reduce_fusion
  200.9 17.5 %all-to-all-done.2 = bf16[32,4,2880]{2,1,0:T(4,128)(2,1)S(1)} async-done(((bf16[32,4,2880]{2,1,0:T(4,128)(2,1)}), bf16[32,4,2880]{2,1,0:T(4,128)(2,1)S(1)}, u32[]{:S(2)}, u32[]{:S(2)}) %all-to-all-start.2) | async-done | bytes 737312 | tf_op jit(solution)/shard_map/all_to_all | solution.py:106
  218.4 1.8 gather_fusion.1
  220.2 1.2 add_convert_fusion
  221.4 0.8 fusion.12
  (36 shorter events, 0.5 us)
Async XLA Ops:
  6.5 133.8 %copy-start = (bf16[1,360,2880]{2,1,0:T(8,128)(2,1)S(1)}, bf16[1,360,2880]{2,1,0:T(8,128)(2,1)}, u32[]{:S(2)}) copy-start(bf16[1,360,2880]{2,1,0:T(8,128)(2,1)} %param.18) | copy-start | bytes 6220804
  6.5 1.0 copy-start.1
  7.6 1.3 copy-start.4
  7.6 1.5 copy-start.5
  50.0 4.9 %copy-start.7 = (f32[1,2,360]{2,1,0:T(2,128)S(1)}, f32[1,2,360]{2,1,0:T(2,128)}, u32[]{:S(2)}) copy-start(f32[1,2,360]{2,1,0:T(2,128)} %param.17) | copy-start | bytes 8644
  50.0 72.8 %all-to-all-start.1 = ((bf16[8,128,2880]{1,2,0:T(8,128)(2,1)}), bf16[8,128,2880]{1,2,0:T(8,128)(2,1)}, u32[]{:S(2)}, u32[]{:S(2)}) async-start(bf16[8,128,2880]{1,2,0:T(8,128)(2,1)} %stack.3), calls=%async_computation.1 | async-start | bytes 11796480 | tf_op jit(solution)/shard_map/all_to_all | solution.py:16
  54.8 130.1 %reduce-scatter.2.cloned.1.call-start = ((), (), s32[]{:S(2)}) async-start(), calls=%async_computation.4 | async-start | bytes 6782976 | tf_op jit(solution)/shard_map/reduce_scatter | solution.py:104
  122.7 14.4 %slice-start = ((s8[4239360]{0:T(1024)(128)(4,1)}), s8[45056]{0:T(1024)(128)(4,1)S(1)}, s32[]{:S(2)}) async-start(s8[4239360]{0:T(1024)(128)(4,1)} %bitcast.38), calls=%async_computation.5 | async-start | bytes 90112
  131.2 6.0 %copy-start.3 = (bf16[8,128,2880]{2,1,0:T(8,128)(2,1)S(1)}, bf16[8,128,2880]{2,1,0:T(8,128)(2,1)}, u32[]{:S(2)}) copy-start(bf16[8,128,2880]{2,1,0:T(8,128)(2,1)} %copy.37) | copy-start | bytes 17694724
  131.2 6.3 %slice-start.1 = ((s8[4239360]{0:T(1024)(128)(4,1)}), s8[4194304]{0:T(1024)(128)(4,1)S(1)}, s32[]{:S(2)}) async-start(s8[4239360]{0:T(1024)(128)(4,1)} %bitcast.38), calls=%async_computation.6 | async-start | bytes 8388608
  145.8 52.0 %copy-start.2 = (f32[32,2880]{1,0:T(8,128)S(1)}, f32[32,2880]{1,0:T(8,128)}, u32[]{:S(2)}) copy-start(f32[32,2880]{1,0:T(8,128)} %param.19) | copy-start | bytes 1105924
  187.3 31.1 %all-to-all-start.2 = ((bf16[32,4,2880]{2,1,0:T(4,128)(2,1)}), bf16[32,4,2880]{2,1,0:T(4,128)(2,1)S(1)}, u32[]{:S(2)}, u32[]{:S(2)}) async-start(bf16[32,4,2880]{2,1,0:T(4,128)(2,1)} %reshape.51), calls=%async_computation.3 | async-start | bytes 1507328 | tf_op jit(solution)/shard_map/all_to_all | solution.py:106
  197.8 1.7 copy-start.8
  197.8 2.9 %copy-start.6 = (s32[16,4]{0,1:T(4,128)S(1)}, s32[16,4]{0,1:T(4,128)}, u32[]{:S(2)}) copy-start(s32[16,4]{0,1:T(4,128)} %param.14) | copy-start | bytes 772
Sparse Core Ops, SparseCore 0:
  145.9 38.9 reduce-scatter.1
